TPU v7x, 32 devices: a whole 2x2x4 slice. The times are simulated.
32 devices in a mesh: dp: 16 (over z, y, x), fsdp: 2 (over core).
Axes of the slice: x: 2, y: 2, z: 4, core: 2. Of those that a mesh axis runs over, the one named last changes fastest.
Arguments:
- tokens: bfloat16 [32, 1024, 768], P(('dp', 'fsdp')), may hold values from -6 to 6
- cotangent: bfloat16 [32, 1024, 768], P(('dp', 'fsdp')), may hold values from -6 to 6
- segments: int32 [32, 1024], P(('dp', 'fsdp')), may hold values from 0 to 15, never falling along the last dimension, each value on 1 to 128 neighbouring positions
- keep_mask: int32 [32, 1024], P(('dp', 'fsdp')), may hold values 0 or 1
- qkv_weight: float32 [2, 768, 2304], P(None, 'fsdp'), may hold values from -0.21875 to 0.21875
- qkv_first: float32 [2, 768, 2304], P(None, 'fsdp'), may hold values from -512 to 512
- qkv_second: float32 [2, 768, 2304], P(None, 'fsdp'), may hold values from 4096 to 65536
- proj_weight: float32 [2, 768, 768], P(None, 'fsdp'), may hold values from -0.625 to 0.625
- proj_first: float32 [2, 768, 768], P(None, 'fsdp'), may hold values from -512 to 512
- proj_second: float32 [2, 768, 768], P(None, 'fsdp'), may hold values from 4096 to 65536
- up_weight: float32 [2, 768, 3072], P(None, 'fsdp'), may hold values from -0.21875 to 0.21875
- up_first: float32 [2, 768, 3072], P(None, 'fsdp'), may hold values from -512 to 512
- up_second: float32 [2, 768, 3072], P(None, 'fsdp'), may hold values from 4096 to 65536
- down_weight: float32 [2, 3072, 768], P(None, 'fsdp'), may hold values from -0.109375 to 0.109375
- down_first: float32 [2, 3072, 768], P(None, 'fsdp'), may hold values from -512 to 512
- down_second: float32 [2, 3072, 768], P(None, 'fsdp'), may hold values from 4096 to 65536
- norm_gains: float32 [2, 768, 4], P(None, 'fsdp'), may hold values from 0.5 to 1.5
- gains_first: float32 [2, 768, 4], P(None, 'fsdp'), may hold values from -512 to 512
- gains_second: float32 [2, 768, 4], P(None, 'fsdp'), may hold values from 4096 to 65536
Outputs:
- output: bfloat16 [32, 1024, 768], P(('dp', 'fsdp'))
- input_grad: float32 [32, 1024, 768], P(('dp', 'fsdp'))
- new_qkv_weight: float32 [2, 768, 2304], P(None, 'fsdp')
- new_qkv_first: float32 [2, 768, 2304], P(None, 'fsdp')
- new_qkv_second: float32 [2, 768, 2304], P(None, 'fsdp')
- new_proj_weight: float32 [2, 768, 768], P(None, 'fsdp')
- new_proj_first: float32 [2, 768, 768], P(None, 'fsdp')
- new_proj_second: float32 [2, 768, 768], P(None, 'fsdp')
- new_up_weight: float32 [2, 768, 3072], P(None, 'fsdp')
- new_up_first: float32 [2, 768, 3072], P(None, 'fsdp')
- new_up_second: float32 [2, 768, 3072], P(None, 'fsdp')
- new_down_weight: float32 [2, 3072, 768], P(None, 'fsdp')
- new_down_first: float32 [2, 3072, 768], P(None, 'fsdp')
- new_down_second: float32 [2, 3072, 768], P(None, 'fsdp')
- new_norm_gains: float32 [2, 768, 4], P(None, 'fsdp')
- new_gains_first: float32 [2, 768, 4], P(None, 'fsdp')
- new_gains_second: float32 [2, 768, 4], P(None, 'fsdp')
Inputs may be any that keep to these rules, and one draw needn't show every extreme that they name: `segments`: in each packed sequence the ids never fall, and each image holds 1 to 128 positions.
All inputs are finite; a program needn't handle non-finite values. No bound on the sum of `keep_mask` on one device may be relied on, other than what follows from the above.
Results may differ from a plain program's by a relative error of at most 0.035.
Values may be sent and summed in bfloat16 or wider, within the bound.
A program may use at most 512 MiB of HBM per device.

v0:
```python
import jax
import jax.numpy as jnp
from jax import lax
from jax.sharding import PartitionSpec as P

D = 768
HEADS = 12
HEAD_DIM = 64
STEP = 5
norm_eps = 1e-06
adam_eps = 1e-08


def layer_norm(values, gain):
    average = jnp.mean(values, axis=-1, keepdims=True)
    centred = values - average
    spread = jnp.mean(centred * centred, axis=-1, keepdims=True)
    return centred * lax.rsqrt(spread + norm_eps) * gain


def gelu_tanh(values):
    return jax.nn.gelu(values, approximate=True)


def allowed_pairs(seg_row, keep_row):
    positions = jnp.arange(seg_row.shape[0])
    diagonal = positions[:, None] == positions[None, :]
    return (seg_row[:, None] == seg_row[None, :]) & ((keep_row[None, :] == 1) | diagonal)


def key_window(start, span, length):
    reach = length // 8
    extent = min(length, span + 2 * reach)
    lower_key = max(0, min(start - reach, length - extent))
    return (lower_key, lower_key + extent)


def block_probs(query_block, keys_part, allowed_block, scale_factor):
    scores = (
        jnp.einsum("qhd,khd->hqk", query_block, keys_part, preferred_element_type=jnp.float32)
        * scale_factor
    )
    return jnp.where(allowed_block[None], scores, -1e30)


def attend_forward(queries, keys_all, values, allowed, span, scale_factor):
    length = queries.shape[0]
    outputs, peaks, totals = ([], [], [])
    for start in range(0, length, span):
        lower_key, upper_key = key_window(start, span, length)
        masked = block_probs(
            queries[start : start + span],
            keys_all[lower_key:upper_key],
            allowed[start : start + span, lower_key:upper_key],
            scale_factor,
        )
        peak = jnp.max(masked, axis=-1, keepdims=True)
        expo = jnp.exp(masked - peak)
        total = jnp.sum(expo, axis=-1, keepdims=True)
        probs = (expo / total).astype(jnp.bfloat16)
        outputs.append(
            jnp.einsum(
                "hqk,khd->qhd",
                probs,
                values[lower_key:upper_key],
                preferred_element_type=jnp.float32,
            ).astype(jnp.bfloat16)
        )
        peaks.append(peak)
        totals.append(total)
    return (jnp.concatenate(outputs, axis=0), peaks, totals)


def attend_backward(
    queries, keys_all, values, allowed, d_attended, peaks, totals, span, scale_factor
):
    length = queries.shape[0]
    d_keys = jnp.zeros(keys_all.shape, jnp.float32)
    d_values = jnp.zeros(values.shape, jnp.float32)
    d_query_parts = []
    for block_index, start in enumerate(range(0, length, span)):
        lower_key, upper_key = key_window(start, span, length)
        keys_part = keys_all[lower_key:upper_key]
        values_part = values[lower_key:upper_key]
        query_block = queries[start : start + span]
        d_block = d_attended[start : start + span]
        masked = block_probs(
            query_block, keys_part, allowed[start : start + span, lower_key:upper_key], scale_factor
        )
        probs_raw = jnp.exp(masked - peaks[block_index]) / totals[block_index]
        probs = probs_raw.astype(jnp.bfloat16)
        d_probs = jnp.einsum(
            "qhd,khd->hqk", d_block, values_part, preferred_element_type=jnp.float32
        )
        d_values = d_values.at[lower_key:upper_key].add(
            jnp.einsum("hqk,qhd->khd", probs, d_block, preferred_element_type=jnp.float32)
        )
        inner = jnp.sum(d_probs * probs_raw, axis=-1, keepdims=True)
        d_scores = (probs_raw * (d_probs - inner)).astype(jnp.bfloat16)
        d_query_parts.append(
            jnp.einsum("hqk,khd->qhd", d_scores, keys_part, preferred_element_type=jnp.float32)
            * scale_factor
        )
        d_keys = d_keys.at[lower_key:upper_key].add(
            jnp.einsum("hqk,qhd->khd", d_scores, query_block, preferred_element_type=jnp.float32)
            * scale_factor
        )
    return (jnp.concatenate(d_query_parts, axis=0), d_keys, d_values)


def layer_forward(hidden, gathered, allowed_rows, span, scale_factor):
    joint_mat, proj_mat, upper_mat, lower_mat, gain_set = gathered
    gains_wide = gain_set.astype(jnp.float32)
    normed = layer_norm(hidden, gains_wide[:, 0]).astype(jnp.bfloat16)
    mixed = jnp.dot(normed, joint_mat, preferred_element_type=jnp.float32)
    split = mixed.reshape(-1, 3, HEADS, HEAD_DIM)
    queries = layer_norm(split[:, 0], gains_wide[:, 2].reshape(HEADS, HEAD_DIM)).astype(
        jnp.bfloat16
    )
    keys_all = layer_norm(split[:, 1], gains_wide[:, 3].reshape(HEADS, HEAD_DIM)).astype(
        jnp.bfloat16
    )
    values = split[:, 2].astype(jnp.bfloat16)
    attended_rows, peak_rows, total_rows = ([], [], [])
    row_out, row_peaks, row_totals = attend_forward(
        queries, keys_all, values, allowed_rows[0], span, scale_factor
    )
    attended_rows.append(row_out)
    peak_rows.append(row_peaks)
    total_rows.append(row_totals)
    attended = attended_rows[0].reshape(-1, HEADS * HEAD_DIM)
    middle = hidden + jnp.dot(attended, proj_mat, preferred_element_type=jnp.float32)
    normed_two = layer_norm(middle, gains_wide[:, 1]).astype(jnp.bfloat16)
    before = jnp.dot(normed_two, upper_mat, preferred_element_type=jnp.float32)
    active = gelu_tanh(before).astype(jnp.bfloat16)
    result = middle + jnp.dot(active, lower_mat, preferred_element_type=jnp.float32)
    saved = (
        hidden,
        normed,
        split,
        queries,
        keys_all,
        values,
        peak_rows,
        total_rows,
        attended,
        middle,
        normed_two,
        before,
        active,
    )
    return (result, saved)


def layer_backward(d_hidden, saved, gathered, allowed_rows, span, scale_factor):
    joint_mat, proj_mat, upper_mat, lower_mat, gain_set = gathered
    gains_wide = gain_set.astype(jnp.float32)
    (
        hidden,
        normed,
        split,
        queries,
        keys_all,
        values,
        peak_rows,
        total_rows,
        attended,
        middle,
        normed_two,
        before,
        active,
    ) = saved
    d_branch = d_hidden.astype(jnp.bfloat16)
    d_lower = jnp.einsum("nf,nd->fd", active, d_branch, preferred_element_type=jnp.float32)
    d_active = jnp.einsum("nd,fd->nf", d_branch, lower_mat, preferred_element_type=jnp.float32)
    unused_gelu, gelu_back = jax.vjp(gelu_tanh, before)
    d_before = gelu_back(d_active)[0].astype(jnp.bfloat16)
    d_upper = jnp.einsum("nd,nf->df", normed_two, d_before, preferred_element_type=jnp.float32)
    d_normed_two = jnp.einsum("nf,df->nd", d_before, upper_mat, preferred_element_type=jnp.float32)
    unused_two, norm_two_back = jax.vjp(layer_norm, middle, gains_wide[:, 1])
    d_middle_part, d_gain_two = norm_two_back(d_normed_two)
    d_middle = d_hidden + d_middle_part
    d_attn = d_middle.astype(jnp.bfloat16)
    d_proj = jnp.einsum("nd,ne->de", attended, d_attn, preferred_element_type=jnp.float32)
    d_attended = jnp.einsum(
        "ne,de->nd", d_attn, proj_mat, preferred_element_type=jnp.float32
    ).astype(jnp.bfloat16)
    d_attended = d_attended.reshape(-1, HEADS, HEAD_DIM)
    query_parts, key_parts, value_parts = ([], [], [])
    d_q_row, d_k_row, d_v_row = attend_backward(
        queries,
        keys_all,
        values,
        allowed_rows[0],
        d_attended,
        peak_rows[0],
        total_rows[0],
        span,
        scale_factor,
    )
    query_parts.append(d_q_row)
    key_parts.append(d_k_row)
    value_parts.append(d_v_row)
    d_queries = query_parts[0]
    d_keys = key_parts[0]
    d_values = value_parts[0]
    unused_query, query_back = jax.vjp(
        layer_norm, split[:, 0], gains_wide[:, 2].reshape(HEADS, HEAD_DIM)
    )
    d_q_raw, d_gain_query = query_back(d_queries)
    unused_key, key_back = jax.vjp(
        layer_norm, split[:, 1], gains_wide[:, 3].reshape(HEADS, HEAD_DIM)
    )
    d_k_raw, d_gain_key = key_back(d_keys)
    d_mixed = (
        jnp.stack([d_q_raw, d_k_raw, d_values], axis=1)
        .reshape(d_hidden.shape[0], -1)
        .astype(jnp.bfloat16)
    )
    d_joint = jnp.einsum("nd,ne->de", normed, d_mixed, preferred_element_type=jnp.float32)
    d_normed = jnp.einsum("ne,de->nd", d_mixed, joint_mat, preferred_element_type=jnp.float32)
    unused_one, norm_one_back = jax.vjp(layer_norm, hidden, gains_wide[:, 0])
    d_input_part, d_gain_one = norm_one_back(d_normed)
    d_gains = jnp.stack(
        [d_gain_one, d_gain_two, d_gain_query.reshape(-1), d_gain_key.reshape(-1)], axis=1
    )
    return (d_middle + d_input_part, (d_joint, d_proj, d_upper, d_lower, d_gains))


def local_shards(masters, layer_index):
    return tuple((weight_arr[layer_index].astype(jnp.bfloat16) for weight_arr in masters))


def per_device(
    tokens,
    cotangent,
    segments,
    keep_mask,
    qkv_weight,
    qkv_first,
    qkv_second,
    proj_weight,
    proj_first,
    proj_second,
    up_weight,
    up_first,
    up_second,
    down_weight,
    down_first,
    down_second,
    norm_gains,
    gains_first,
    gains_second,
):
    masters = (qkv_weight, proj_weight, up_weight, down_weight, norm_gains)
    firsts = (qkv_first, proj_first, up_first, down_first, gains_first)
    seconds = (qkv_second, proj_second, up_second, down_second, gains_second)
    packs, length, width = tokens.shape
    layers = qkv_weight.shape[0]
    span = min(512, length)
    scale_factor = HEAD_DIM ** (-0.5)
    allowed_rows = [allowed_pairs(segments[0], keep_mask[0])]
    hidden = tokens.reshape(-1, width).astype(jnp.float32)
    stored, held = ([], [])
    for layer_index in range(layers):
        shards = local_shards(masters, layer_index)
        gathered = (
            lax.all_gather(shards[0], "fsdp", axis=0, tiled=True),
            lax.all_gather(shards[1], "fsdp", axis=0, tiled=True),
            lax.all_gather(shards[2], "fsdp", axis=0, tiled=True),
            lax.all_gather(shards[3], "fsdp", axis=0, tiled=True),
            lax.all_gather(shards[4], "fsdp", axis=0, tiled=True),
        )
        hidden, saved = layer_forward(hidden, gathered, allowed_rows, span, scale_factor)
        stored.append(saved)
        held.append(gathered)
    output = hidden.astype(jnp.bfloat16).reshape(tokens.shape)
    d_hidden = cotangent.reshape(-1, width).astype(jnp.float32)
    layer_grads = [None] * layers
    for layer_index in reversed(range(layers)):
        shards = local_shards(masters, layer_index)
        gathered = (
            lax.all_gather(shards[0], "fsdp", axis=0, tiled=True),
            lax.all_gather(shards[1], "fsdp", axis=0, tiled=True),
            lax.all_gather(shards[2], "fsdp", axis=0, tiled=True),
            lax.all_gather(shards[3], "fsdp", axis=0, tiled=True),
            lax.all_gather(shards[4], "fsdp", axis=0, tiled=True),
        )
        d_hidden, grads = layer_backward(
            d_hidden, stored[layer_index], gathered, allowed_rows, span, scale_factor
        )
        layer_grads[layer_index] = grads
    stacked = tuple(
        (
            jnp.stack([layer_grads[layer_index][kind_index] for layer_index in range(layers)])
            for kind_index in range(5)
        )
    )
    shares = (
        lax.psum_scatter(
            stacked[0].astype(jnp.bfloat16), "fsdp", scatter_dimension=1, tiled=True
        ).astype(jnp.float32),
        lax.psum_scatter(
            stacked[1].astype(jnp.bfloat16), "fsdp", scatter_dimension=1, tiled=True
        ).astype(jnp.float32),
        lax.psum_scatter(
            stacked[2].astype(jnp.bfloat16), "fsdp", scatter_dimension=1, tiled=True
        ).astype(jnp.float32),
        lax.psum_scatter(
            stacked[3].astype(jnp.bfloat16), "fsdp", scatter_dimension=1, tiled=True
        ).astype(jnp.float32),
        lax.psum_scatter(
            stacked[4].astype(jnp.bfloat16), "fsdp", scatter_dimension=1, tiled=True
        ).astype(jnp.float32),
    )
    summed = (
        lax.psum(shares[0].astype(jnp.bfloat16), "dp").astype(jnp.float32),
        lax.psum(shares[1].astype(jnp.bfloat16), "dp").astype(jnp.float32),
        lax.psum(shares[2].astype(jnp.bfloat16), "dp").astype(jnp.float32),
        lax.psum(shares[3].astype(jnp.bfloat16), "dp").astype(jnp.float32),
        lax.psum(shares[4].astype(jnp.bfloat16), "dp").astype(jnp.float32),
    )
    corr_one = 1.0 - 0.5**STEP
    corr_two = 1.0 - 0.5**STEP
    updated = []
    for kind_index in range(5):
        grad_now = summed[kind_index]
        first_new = 0.5 * firsts[kind_index] + 0.5 * grad_now
        second_new = 0.5 * seconds[kind_index] + 0.5 * grad_now * grad_now
        rate_now = 0.5 if kind_index == 4 else D ** (-0.5)
        decay_now = 0.0 if kind_index == 4 else 0.1
        weight_old = masters[kind_index]
        weight_new = weight_old - rate_now * (
            first_new / corr_one / (jnp.sqrt(second_new / corr_two) + adam_eps)
            + decay_now * weight_old
        )
        updated.append((weight_new, first_new, second_new))
    input_grad = d_hidden.reshape(tokens.shape)
    return (
        output,
        input_grad,
        updated[0][0],
        updated[0][1],
        updated[0][2],
        updated[1][0],
        updated[1][1],
        updated[1][2],
        updated[2][0],
        updated[2][1],
        updated[2][2],
        updated[3][0],
        updated[3][1],
        updated[3][2],
        updated[4][0],
        updated[4][1],
        updated[4][2],
    )


def solution(mesh):
    placed = (
        P(("dp", "fsdp"), None, None),
        P(("dp", "fsdp"), None, None),
        P(("dp", "fsdp"), None),
        P(("dp", "fsdp"), None),
        P(None, "fsdp", None),
        P(None, "fsdp", None),
        P(None, "fsdp", None),
        P(None, "fsdp", None),
        P(None, "fsdp", None),
        P(None, "fsdp", None),
        P(None, "fsdp", None),
        P(None, "fsdp", None),
        P(None, "fsdp", None),
        P(None, "fsdp", None),
        P(None, "fsdp", None),
        P(None, "fsdp", None),
        P(None, "fsdp", None),
        P(None, "fsdp", None),
        P(None, "fsdp", None),
    )
    return jax.shard_map(
        per_device,
        mesh=mesh,
        in_specs=placed,
        out_specs=(
            P(("dp", "fsdp"), None, None),
            P(("dp", "fsdp"), None, None),
            P(None, "fsdp", None),
            P(None, "fsdp", None),
            P(None, "fsdp", None),
            P(None, "fsdp", None),
            P(None, "fsdp", None),
            P(None, "fsdp", None),
            P(None, "fsdp", None),
            P(None, "fsdp", None),
            P(None, "fsdp", None),
            P(None, "fsdp", None),
            P(None, "fsdp", None),
            P(None, "fsdp", None),
            P(None, "fsdp", None),
            P(None, "fsdp", None),
            P(None, "fsdp", None),
        ),
        check_vma=False,
    )
```

profile of v0, /device:TPU:0, one launch (start us, length us, event | category | flops | bytes accessed | tf_op | source)
XLA Modules:
  0.0 1156.6 jit_solution(5405106433137993365)
XLA Ops:
  83.4 23.9 %fusion.235 = (f32[12,512]{1,0:T(8,128)S(1)}, f32[12,512,768]{2,1,0:T(8,128)}) fusion(f32[12,512,768]{2,1,0:T(8,128)} %fusion.181, pred[512,768]{1,0:T(8,128)(4,1)S(1)} %copy-done.91), kind=kOutput, calls=%fused_computation.379 | output fusion | flops 28312320 | bytes 38166528 | tf_op jit(solution)/shard_map/sub | solution.py:58
  107.3 23.4 %fusion.236 = (f32[12,512]{1,0:T(8,128)S(1)}, f32[12,512,768]{2,1,0:T(8,128)}) fusion(f32[12,512,768]{2,1,0:T(8,128)} %fusion.184, pred[512,768]{1,0:T(8,128)(4,1)S(1)} %get-tuple-element.220), kind=kOutput, calls=%fused_computation.380 | output fusion | flops 28312320 | bytes 38166528 | tf_op jit(solution)/shard_map/sub | solution.py:58
  156.2 11.1 fusion.51
  167.4 12.1 %fusion.238 = (f32[1024]{0:T(1024)S(1)}, f32[1024,768]{0,1:T(8,128)S(1)}) fusion(f32[1024,768]{0,1:T(8,128)S(1)} %copy-done.6, bf16[1,3072,768]{2,1,0:T(8,128)(2,1)} %all-gather.25.cloned.1.call-done, f32[1024,3072]{1,0:T(8,128)} %fusion.51), kind=kOutput, calls=%fused_computation.382 | convolution fusion | flops 4861721600 | bytes 23597056 | tf_op jit(solution)/shard_map/dot_general | solution.py:136
  212.0 23.5 %fusion.239 = (f32[12,512]{1,0:T(8,128)S(1)}, f32[12,512,768]{2,1,0:T(8,128)}) fusion(f32[12,512,768]{2,1,0:T(8,128)} %fusion.175, pred[512,768]{1,0:T(8,128)(4,1)S(1)} %copy-done.92), kind=kOutput, calls=%fused_computation.383 | output fusion | flops 28312320 | bytes 38166528 | tf_op jit(solution)/shard_map/sub | solution.py:58
  235.5 23.6 %fusion.240 = (f32[12,512]{1,0:T(8,128)S(1)}, f32[12,512,768]{2,1,0:T(8,128)}) fusion(f32[12,512,768]{2,1,0:T(8,128)} %fusion.178, pred[512,768]{1,0:T(8,128)(4,1)S(1)} %get-tuple-element.220), kind=kOutput, calls=%fused_computation.384 | output fusion | flops 28312320 | bytes 38166528 | tf_op jit(solution)/shard_map/sub | solution.py:58
  293.0 15.7 %fusion.21 = bf16[1024,3072]{1,0:T(8,128)(2,1)S(1)} fusion(f32[1024,3072]{1,0:T(8,128)} %fusion.43, bf16[1,3072,768]{2,1,0:T(8,128)(2,1)} %all-gather.33.cloned.1.call-done, bf16[1,1024,768]{2,1,0:T(8,128)(2,1)} %param.36), kind=kOutput, calls=%fused_computation.45 | convolution fusion | flops 4894752768 | bytes 25165824 | tf_op jit(solution)/shard_map/nd,fd->nf/dot_general | solution.py:175
  327.9 15.0 %multiply_reduce_fusion.3 = (f32[12,512]{1,0:T(8,128)S(1)}, f32[12,512,768]{2,1,0:T(8,128)}) fusion(f32[12,512,768]{2,1,0:T(8,128)} %get-tuple-element.237, f32[12,512]{1,0:T(8,128)S(1)} %copy-done.135, bf16[512,12,64]{0,2,1:T(8,128)(2,1)S(1)} %bitcast.379, bf16[1024,3,12,64]{0,3,2,1:T(8,128)(2,1)S(1)} %bitcast.359), kind=kOutput, calls=%fused_computation.11 | convolution fusion | flops 618129408 | bytes 39772160 | tf_op jit(solution)/shard_map/qhd,khd->hqk/dot_general | solution.py:92
  342.9 13.2 %multiply_convert_fusion.3 = bf16[12,512,768]{2,1,0:T(8,128)(2,1)S(1)} fusion(f32[12,512,768]{2,1,0:T(8,128)} %get-tuple-element.242, f32[12,512]{1,0:T(8,128)S(1)} %get-tuple-element.241, f32[12,512,768]{2,1,0:T(8,128)} %get-tuple-element.237, f32[12,512]{1,0:T(8,128)S(1)} %copy-done.135), kind=kLoop, calls=%fused_computation.10 | loop fusion | flops 18874368 | bytes 47235072 | tf_op jit(solution)/shard_map/convert_element_type | solution.py:99
  362.9 15.1 %multiply_reduce_fusion.2 = (f32[12,512]{1,0:T(8,128)S(1)}, f32[12,512,768]{2,1,0:T(8,128)}) fusion(f32[12,512,768]{2,1,0:T(8,128)} %get-tuple-element.235, f32[12,512]{1,0:T(8,128)S(1)} %copy-done.133, bf16[512,12,64]{0,2,1:T(8,128)(2,1)S(1)} %bitcast.376, bf16[1024,3,12,64]{0,3,2,1:T(8,128)(2,1)S(1)} %bitcast.359), kind=kOutput, calls=%fused_computation.9 | convolution fusion | flops 618129408 | bytes 39772160 | tf_op jit(solution)/shard_map/qhd,khd->hqk/dot_general | solution.py:92
  387.6 12.8 %multiply_convert_fusion.2 = bf16[12,512,768]{2,1,0:T(8,128)(2,1)S(1)} fusion(f32[12,512,768]{2,1,0:T(8,128)} %get-tuple-element.244, f32[12,512]{1,0:T(8,128)S(1)} %get-tuple-element.243, f32[12,512,768]{2,1,0:T(8,128)} %get-tuple-element.235, f32[12,512]{1,0:T(8,128)S(1)} %copy-done.133), kind=kLoop, calls=%fused_computation.8 | loop fusion | flops 18874368 | bytes 47235072 | tf_op jit(solution)/shard_map/convert_element_type | solution.py:99
  430.3 18.2 %fusion.14 = bf16[1024,3072]{1,0:T(8,128)(2,1)} fusion(f32[1024,3072]{1,0:T(8,128)} %fusion.51, bf16[1,3072,768]{2,1,0:T(8,128)(2,1)S(1)} %bitcast.384, f32[1024,768]{0,1:T(8,128)S(1)} %add_add_fusion.11), kind=kOutput, calls=%fused_computation.38 | convolution fusion | flops 4895539200 | bytes 26738688 | tf_op jit(solution)/shard_map/nd,fd->nf/dot_general | solution.py:175
  469.8 12.2 %multiply_reduce_fusion.1 = (f32[12,512]{1,0:T(8,128)S(1)}, f32[12,512,768]{2,1,0:T(8,128)}) fusion(f32[12,512,768]{2,1,0:T(8,128)} %get-tuple-element.229, f32[12,512]{1,0:T(8,128)S(1)} %copy-done.131, bf16[512,12,64]{0,2,1:T(8,128)(2,1)S(1)} %bitcast.381, bf16[1024,3,12,64]{0,3,2,1:T(8,128)(2,1)} %get-tuple-element.224), kind=kOutput, calls=%fused_computation.7 | convolution fusion | flops 618129408 | bytes 39763968 | tf_op jit(solution)/shard_map/qhd,khd->hqk/dot_general | solution.py:92
  482.1 12.8 %multiply_convert_fusion.1 = bf16[12,512,768]{2,1,0:T(8,128)(2,1)S(1)} fusion(f32[12,512,768]{2,1,0:T(8,128)} %get-tuple-element.249, f32[12,512]{1,0:T(8,128)S(1)} %get-tuple-element.248, f32[12,512,768]{2,1,0:T(8,128)} %get-tuple-element.229, f32[12,512]{1,0:T(8,128)S(1)} %copy-done.131), kind=kLoop, calls=%fused_computation.6 | loop fusion | flops 18874368 | bytes 47235072 | tf_op jit(solution)/shard_map/convert_element_type | solution.py:99
  505.7 15.2 %multiply_reduce_fusion = (f32[12,512]{1,0:T(8,128)S(1)}, f32[12,512,768]{2,1,0:T(8,128)}) fusion(f32[12,512,768]{2,1,0:T(8,128)} %get-tuple-element.227, f32[12,512]{1,0:T(8,128)S(1)} %copy-done.129, bf16[512,12,64]{0,2,1:T(8,128)(2,1)S(1)} %bitcast.374, bf16[1024,3,12,64]{0,3,2,1:T(8,128)(2,1)} %get-tuple-element.224), kind=kOutput, calls=%fused_computation.5 | convolution fusion | flops 618129408 | bytes 39763968 | tf_op jit(solution)/shard_map/qhd,khd->hqk/dot_general | solution.py:92
  520.9 16.5 %multiply_convert_fusion = bf16[12,512,768]{2,1,0:T(8,128)(2,1)} fusion(f32[12,512,768]{2,1,0:T(8,128)} %get-tuple-element.251, f32[12,512]{1,0:T(8,128)S(1)} %get-tuple-element.250, f32[12,512,768]{2,1,0:T(8,128)} %get-tuple-element.227, f32[12,512]{1,0:T(8,128)S(1)} %copy-done.129), kind=kLoop, calls=%fused_computation.4 | loop fusion | flops 18874368 | bytes 47235072 | tf_op jit(solution)/shard_map/convert_element_type | solution.py:99
  578.8 13.8 %fusion.73 = bf16[1,3072,768]{2,1,0:T(8,128)(2,1)} fusion(f32[1024,768]{0,1:T(8,128)} %copy-done.13, f32[1024,3072]{1,0:T(8,128)} %fusion.51), kind=kOutput, calls=%fused_computation.132 | convolution fusion | flops 4863295488 | bytes 20447232 | tf_op jit(solution)/shard_map/nf,nd->fd/dot_general | solution.py:174
  592.6 11.9 %fusion.74 = bf16[1,3072,768]{2,1,0:T(8,128)(2,1)} fusion(bf16[1,1024,768]{2,1,0:T(8,128)(2,1)S(1)} %copy-done.53, f32[1024,3072]{1,0:T(8,128)} %fusion.43), kind=kOutput, calls=%fused_computation.133 | convolution fusion | flops 4862509056 | bytes 18874368 | tf_op jit(solution)/shard_map/nf,nd->fd/dot_general | solution.py:174
  623.9 11.2 fusion.71
  687.7 45.7 %psum.39 = bf16[2,384,4]{1,2,0:T(4,128)(2,1)S(1)} all-reduce(bf16[2,384,4]{1,2,0:T(4,128)(2,1)S(1)} %copy.57), channel_id=1, replica_groups=mesh['dp'=16,'fsdp'=2] {'dp'}, use_global_device_ids=true, to_apply=%region_61.62 | all-reduce | flops 3072 | bytes 12288 | tf_op jit(solution)/shard_map/psum | solution.py:321
  734.0 346.8 %all-reduce.7.cloned.1.call-done = (bf16[2,384,2304]{2,1,0:T(8,128)(2,1)}, bf16[2,384,768]{2,1,0:T(8,128)(2,1)}, bf16[2,384,3072]{2,1,0:T(8,128)(2,1)}, bf16[2,1536,768]{2,1,0:T(8,128)(2,1)}) async-done(((bf16[2,384,2304]{2,1,0:T(8,128)(2,1)}, bf16[2,384,768]{2,1,0:T(8,128)(2,1)}, bf16[2,384,3072]{2,1,0:T(8,128)(2,1)}, bf16[2,1536,768]{2,1,0:T(8,128)(2,1)}), (bf16[2,384,2304]{2,1,0:T(8,128)(2,1)}, ...) | async-done | bytes 14155792 | tf_op jit(solution)/shard_map/psum | solution.py:317
  1087.7 18.0 %multiply_subtract_fusion.2 = (f32[2,384,2304]{2,1,0:T(8,128)}, f32[2,384,2304]{2,1,0:T(8,128)}, f32[2,384,2304]{2,1,0:T(8,128)}) fusion(f32[2,384,2304]{2,1,0:T(8,128)} %param.39, bf16[2,384,2304]{2,1,0:T(8,128)(2,1)} %get-tuple-element.181, f32[2,384,2304]{2,1,0:T(8,128)} %param.40, f32[2,384,2304]{2,1,0:T(8,128)} %param.41), kind=kLoop, calls=%fused_computation.75 | loop fusion | flops 26542080 | bytes 46006272 | tf_op jit(solution)/shard_map/sub | solution.py:333
  1105.7 20.7 %multiply_subtract_fusion.1 = (f32[2,384,3072]{2,1,0:T(8,128)}, f32[2,384,3072]{2,1,0:T(8,128)}, f32[2,384,3072]{2,1,0:T(8,128)}) fusion(f32[2,384,3072]{2,1,0:T(8,128)S(1)} %bitcast.339, bf16[2,384,3072]{2,1,0:T(8,128)(2,1)} %get-tuple-element.183, f32[2,384,3072]{2,1,0:T(8,128)} %param.46, f32[2,384,3072]{2,1,0:T(8,128)} %param.47), kind=kLoop, calls=%fused_computation.56 | loop fusion | flops 35389440 | bytes 61341696 | tf_op jit(solution)/shard_map/sub | solution.py:333
  1126.4 23.4 %multiply_subtract_fusion = (f32[2,1536,768]{2,1,0:T(8,128)}, f32[2,1536,768]{2,1,0:T(8,128)}, f32[2,1536,768]{2,1,0:T(8,128)}) fusion(f32[2,1536,768]{2,1,0:T(8,128)} %param.48, bf16[2,1536,768]{2,1,0:T(8,128)(2,1)} %get-tuple-element.184, f32[2,1536,768]{2,1,0:T(8,128)} %param.49, f32[2,1536,768]{2,1,0:T(8,128)} %param.50), kind=kLoop, calls=%fused_computation.55 | loop fusion | flops 35389440 | bytes 61341696 | tf_op jit(solution)/shard_map/sub | solution.py:333
  (566 shorter events, 384.3 us)
Async XLA Ops:
  7.2 38.6 %all-gather.19.cloned.1.call-start = ((), (), s32[]{:S(2)}) async-start(), calls=%async_computation.9 | async-start | bytes 5308416 | tf_op jit(solution)/shard_map/all_gather | solution.py:268
  12.6 137.5 %all-gather.21.cloned.1.call-start = ((), (), s32[]{:S(2)}) async-start(), calls=%async_computation.10 | async-start | bytes 1769472 | tf_op jit(solution)/shard_map/all_gather | solution.py:269
  14.6 141.6 %all-gather.23.cloned.1.call-start = ((), (), s32[]{:S(2)}) async-start(), calls=%async_computation.11 | async-start | bytes 7077888 | tf_op jit(solution)/shard_map/all_gather | solution.py:270
  21.6 145.8 %all-gather.25.cloned.1.call-start = ((), (), s32[]{:S(2)}) async-start(), calls=%async_computation.12 | async-start | bytes 7077888 | tf_op jit(solution)/shard_map/all_gather | solution.py:271
  29.6 152.0 %all-gather.27.cloned.1.call-start = ((), (), s32[]{:S(2)}) async-start(), calls=%async_computation.13 | async-start | bytes 5308416 | tf_op jit(solution)/shard_map/all_gather | solution.py:268
  30.2 247.0 %all-gather.29.cloned.1.call-start = ((), (), s32[]{:S(2)}) async-start(), calls=%async_computation.14 | async-start | bytes 1769472 | tf_op jit(solution)/shard_map/all_gather | solution.py:269
  30.7 251.1 %all-gather.31.cloned.1.call-start = ((), (), s32[]{:S(2)}) async-start(), calls=%async_computation.15 | async-start | bytes 7077888 | tf_op jit(solution)/shard_map/all_gather | solution.py:270
  31.5 261.4 %all-gather.33.cloned.1.call-start = ((), (), s32[]{:S(2)}) async-start(), calls=%async_computation.16 | async-start | bytes 7077888 | tf_op jit(solution)/shard_map/all_gather | solution.py:271
  32.3 623.6 %reduce-scatter.10.cloned.1.call-start = ((), (), s32[]{:S(2)}) async-start(), calls=%async_computation.6 | async-start | bytes 3538944 | tf_op jit(solution)/shard_map/reduce_scatter | solution.py:303
  37.8 118.4 %copy-start.83 = (f32[768]{0:T(1024)}, f32[768]{0:T(1024)S(1)}, u32[]{:S(2)}) copy-start(f32[768]{0:T(1024)S(1)} %get-tuple-element.177) | copy-start | bytes 9220
  42.2 108.0 %copy-start.2 = (bf16[1,1024,768]{1,2,0:T(8,128)(2,1)}, bf16[1,1024,768]{1,2,0:T(8,128)(2,1)S(1)}, u32[]{:S(2)}) copy-start(bf16[1,1024,768]{1,2,0:T(8,128)(2,1)S(1)} %copy.44) | copy-start | bytes 4718596
  281.4 33.5 %copy-start.4 = (f32[1024,768]{0,1:T(8,128)}, f32[1024,768]{0,1:T(8,128)S(1)}, u32[]{:S(2)}) copy-start(f32[1024,768]{0,1:T(8,128)S(1)} %get-tuple-element.239) | copy-start | bytes 9437188
  281.4 33.4 %copy-start.79 = (f32[1024]{0:T(1024)}, f32[1024]{0:T(1024)S(1)}, u32[]{:S(2)}) copy-start(f32[1024]{0:T(1024)S(1)} %broadcast_multiply_fusion.4) | copy-start | bytes 12292
  502.6 153.3 %reduce-scatter.8.cloned.1.call-start = ((), (), s32[]{:S(2)}) async-start(), calls=%async_computation.5 | async-start | bytes 10616832 | tf_op jit(solution)/shard_map/reduce_scatter | solution.py:300
  505.7 38.5 %slice-start.3 = ((s8[9437184]{0:T(1024)(128)(4,1)}), s8[4194304]{0:T(1024)(128)(4,1)S(1)}, s32[]{:S(2)}) async-start(s8[9437184]{0:T(1024)(128)(4,1)} %bitcast.334), calls=%async_computation.22 | async-start | bytes 8388608
  505.7 38.5 %slice-start.4 = ((s8[9437184]{0:T(1024)(128)(4,1)}), s8[1048576]{0:T(1024)(128)(4,1)S(1)}, s32[]{:S(2)}) async-start(s8[9437184]{0:T(1024)(128)(4,1)} %bitcast.334), calls=%async_computation.23 | async-start | bytes 2097152
  578.7 77.2 %reduce-scatter.14.cloned.1.call-start = ((), (), s32[]{:S(2)}) async-start(), calls=%async_computation.8 | async-start | bytes 14155776 | tf_op jit(solution)/shard_map/reduce_scatter | solution.py:309
  613.0 50.1 %reduce-scatter.12.cloned.1.call-start = ((), (), s32[]{:S(2)}) async-start(), calls=%async_computation.7 | async-start | bytes 14155776 | tf_op jit(solution)/shard_map/reduce_scatter | solution.py:306
  643.5 43.0 %reduce-scatter.16.cloned.1.call-start = ((), (), s32[]{:S(2)}) async-start(), calls=%async_computation.17 | async-start | bytes 294912
  655.8 425.0 %all-reduce.7.cloned.1.call-start = ((), (), s32[]{:S(2)}) async-start(), calls=%async_computation.18 | async-start | bytes 28311552 | tf_op jit(solution)/shard_map/psum | solution.py:317
  682.8 50.5 %copy-start.107 = (f32[2,384,4]{1,2,0:T(4,128)S(1)}, f32[2,384,4]{1,2,0:T(4,128)}, u32[]{:S(2)}) copy-start(f32[2,384,4]{1,2,0:T(4,128)} %param.51) | copy-start | bytes 36868
  682.8 50.6 %copy-start.139 = (f32[2,384,4]{1,2,0:T(4,128)S(1)}, f32[2,384,4]{1,2,0:T(4,128)}, u32[]{:S(2)}) copy-start(f32[2,384,4]{1,2,0:T(4,128)} %param.52) | copy-start | bytes 36868
  682.8 50.6 %copy-start.140 = (f32[2,384,4]{1,2,0:T(4,128)S(1)}, f32[2,384,4]{1,2,0:T(4,128)}, u32[]{:S(2)}) copy-start(f32[2,384,4]{1,2,0:T(4,128)} %param.53) | copy-start | bytes 36868
  682.8 398.0 %copy-start.34 = (f32[2,384,768]{2,1,0:T(8,128)S(1)}, f32[2,384,768]{2,1,0:T(8,128)}, u32[]{:S(2)}) copy-start(f32[2,384,768]{2,1,0:T(8,128)} %param.42) | copy-start | bytes 7077892
  (169 other events, 1050.7 us)
Sparse Core Ops, SparseCore 0:
  12.8 15.3 all-gather.18
  30.3 10.3 all-gather.20
  42.9 15.5 all-gather.22
  60.5 15.5 all-gather.24
  78.1 13.8 all-gather.26
  94.0 10.3 all-gather.28
  106.5 15.5 all-gather.30
  124.3 15.5 all-gather.32
  502.7 11.6 reduce-scatter.9
  578.8 17.2 reduce-scatter.7
  613.1 19.5 reduce-scatter.13
  643.6 19.4 reduce-scatter.11
  665.9 8.8 reduce-scatter.15
  681.1 399.6 all-reduce.6
where the time goes:
time: 1160 us
  matrix products  364 us (31%)
  waiting for transfers between devices  357 us (31%)
  other arithmetic  302 us (26%)
  local copies, waits for them, and re-layouts  66.4 us (6%)
  blocking collectives  49.7 us (4%)
  between operations  16.6 us (1%)
    psum x1, waiting for transfers between devices, per_device(): lax.psum(shares[0].astype(jnp.bfloat16), 'dp').astype(jnp.float32)  347 us
    sub x4, other arithmetic, attend_forward(): expo = jnp.exp(masked - peak)  94.3 us
    sub x5, other arithmetic, per_device(): weight_old - rate_now * (first_new / corr_one / (jnp.sqrt(second_new / co...  69.6 us
    dot_general x4, matrix products, attend_backward(): jnp.einsum('qhd,khd->hqk', d_block, values_part, preferred_element_type=j...  57.5 us
    convert_element_type x4, other arithmetic, attend_backward(): d_scores = (probs_raw * (d_probs - inner)).astype(jnp.bfloat16)  55.3 us
    psum x1, blocking collectives, per_device(): lax.psum(shares[4].astype(jnp.bfloat16), 'dp').astype(jnp.float32)  45.7 us
    unnamed x366, local copies, waits for them, and re-layouts  42.8 us
    dot_general x2, matrix products, layer_backward(): jnp.einsum('nd,fd->nf', d_branch, lower_mat, preferred_element_type=jnp.f...  33.9 us
  transfers between devices with their start and end apart: 14, of which 2 were waited for; matrix products, arithmetic and copies ran while one was open for 37% of the time, Pallas kernels for 0%

commit v1 on v0

--- a/solution.py
+++ b/solution.py
@@ -314,7 +314,9 @@
         ).astype(jnp.float32),
     )
     summed = (
-        lax.psum(shares[0].astype(jnp.bfloat16), "dp").astype(jnp.float32),
+        jnp.sum(lax.all_gather(shares[0].astype(jnp.bfloat16), axis_name="dp"), axis=0).astype(
+            jnp.float32
+        ),
         lax.psum(shares[1].astype(jnp.bfloat16), "dp").astype(jnp.float32),
         lax.psum(shares[2].astype(jnp.bfloat16), "dp").astype(jnp.float32),
         lax.psum(shares[3].astype(jnp.bfloat16), "dp").astype(jnp.float32),

time: 1160 us -> 1620 us (1.40)
  waiting for transfers between devices: 357 us -> 788 us
  other arithmetic: 302 us -> 325 us
    all_gather x0 -> x1, waiting for transfers between devices: none -> 518 us  [per_device(): lax.all_gather(shares[0].astype(jnp.bfloat16), axis_name='dp')]
    psum x1, waiting for transfers between devices: 347 us -> 262 us  [per_device(): lax.psum(shares[1].astype(jnp.bfloat16), 'dp').astype(jnp.float32)]
    reduce_sum x0 -> x1, other arithmetic: none -> 19 us  [per_device(): jnp.sum(lax.all_gather(shares[0].astype(jnp.bfloat16), axis_name='dp'), a...]
    unnamed x366 -> x350, local copies, waits for them, and re-layouts: 42.8 us -> 44 us
  transfers between devices with their start and end apart: 14 -> 15, of which waited for: 2 -> 3; matrix products, arithmetic and copies ran while one was open for 37% -> 33% of each run, Pallas kernels for 0% -> 0%
where the time goes in v1:
time: 1620 us; the launch traced here: 1610 us
  waiting for transfers between devices  788 us (49%)
  matrix products  368 us (23%)
  other arithmetic  325 us (20%)
  local copies, waits for them, and re-layouts  66.1 us (4%)
  blocking collectives  49.7 us (3%)
  between operations  16.5 us (1%)
    all_gather x1, waiting for transfers between devices, per_device(): lax.all_gather(shares[0].astype(jnp.bfloat16), axis_name='dp')  518 us
    psum x1, waiting for transfers between devices, per_device(): lax.psum(shares[1].astype(jnp.bfloat16), 'dp').astype(jnp.float32)  262 us
    sub x4, other arithmetic, attend_forward(): expo = jnp.exp(masked - peak)  94.4 us
    sub x5, other arithmetic, per_device(): weight_old - rate_now * (first_new / corr_one / (jnp.sqrt(second_new / co...  69.3 us
    convert_element_type x4, other arithmetic, attend_backward(): d_scores = (probs_raw * (d_probs - inner)).astype(jnp.bfloat16)  58.2 us
    dot_general x4, matrix products, attend_backward(): jnp.einsum('qhd,khd->hqk', d_block, values_part, preferred_element_type=j...  55.9 us
    psum x1, blocking collectives, per_device(): lax.psum(shares[4].astype(jnp.bfloat16), 'dp').astype(jnp.float32)  45.6 us
    unnamed x350, local copies, waits for them, and re-layouts  44 us
  transfers between devices with their start and end apart: 15, of which 3 were waited for; matrix products, arithmetic and copies ran while one was open for 33% of the time, Pallas kernels for 0%

profile of v1, /device:TPU:0, one launch (start us, length us, event | category | flops | bytes accessed | tf_op | source)
XLA Modules:
  0.0 1614.3 jit_solution(14598329960546203916)
XLA Ops:
  83.5 23.9 %fusion.235 = (f32[12,512]{1,0:T(8,128)S(1)}, f32[12,512,768]{2,1,0:T(8,128)}) fusion(f32[12,512,768]{2,1,0:T(8,128)} %fusion.181, pred[512,768]{1,0:T(8,128)(4,1)S(1)} %copy-done.90), kind=kOutput, calls=%fused_computation.379 | output fusion | flops 28312320 | bytes 38166528 | tf_op jit(solution)/shard_map/sub | solution.py:58
  107.4 23.5 %fusion.236 = (f32[12,512]{1,0:T(8,128)S(1)}, f32[12,512,768]{2,1,0:T(8,128)}) fusion(f32[12,512,768]{2,1,0:T(8,128)} %fusion.184, pred[512,768]{1,0:T(8,128)(4,1)S(1)} %get-tuple-element.219), kind=kOutput, calls=%fused_computation.380 | output fusion | flops 28312320 | bytes 38166528 | tf_op jit(solution)/shard_map/sub | solution.py:58
  167.5 12.1 fusion.238
  212.2 23.3 %fusion.239 = (f32[12,512]{1,0:T(8,128)S(1)}, f32[12,512,768]{2,1,0:T(8,128)}) fusion(f32[12,512,768]{2,1,0:T(8,128)} %fusion.175, pred[512,768]{1,0:T(8,128)(4,1)S(1)} %copy-done.91), kind=kOutput, calls=%fused_computation.383 | output fusion | flops 28312320 | bytes 38166528 | tf_op jit(solution)/shard_map/sub | solution.py:58
  235.5 23.7 %fusion.240 = (f32[12,512]{1,0:T(8,128)S(1)}, f32[12,512,768]{2,1,0:T(8,128)}) fusion(f32[12,512,768]{2,1,0:T(8,128)} %fusion.178, pred[512,768]{1,0:T(8,128)(4,1)S(1)} %get-tuple-element.219), kind=kOutput, calls=%fused_computation.384 | output fusion | flops 28312320 | bytes 38166528 | tf_op jit(solution)/shard_map/sub | solution.py:58
  293.1 15.7 fusion.21
  328.0 15.1 multiply_reduce_fusion.3
  343.1 13.2 multiply_convert_fusion.3
  363.1 15.1 multiply_reduce_fusion.2
  387.8 12.8 multiply_convert_fusion.2
  430.5 17.9 %fusion.14 = bf16[1024,3072]{1,0:T(8,128)(2,1)} fusion(f32[1024,3072]{1,0:T(8,128)} %fusion.51, bf16[1,3072,768]{2,1,0:T(8,128)(2,1)S(1)} %bitcast.382, f32[1024,768]{0,1:T(8,128)S(1)} %add_add_fusion.11), kind=kOutput, calls=%fused_computation.38 | convolution fusion | flops 4895539200 | bytes 26738688 | tf_op jit(solution)/shard_map/nd,fd->nf/dot_general | solution.py:175
  463.7 14.1 fusion.73
  477.8 11.6 fusion.74
  530.0 12.3 multiply_reduce_fusion.1
  542.4 15.7 multiply_convert_fusion.1
  575.5 13.5 multiply_reduce_fusion
  589.0 16.6 %multiply_convert_fusion = bf16[12,512,768]{2,1,0:T(8,128)(2,1)} fusion(f32[12,512,768]{2,1,0:T(8,128)} %get-tuple-element.250, f32[12,512]{1,0:T(8,128)S(1)} %get-tuple-element.249, f32[12,512,768]{2,1,0:T(8,128)} %get-tuple-element.226, f32[12,512]{1,0:T(8,128)S(1)} %copy-done.128), kind=kLoop, calls=%fused_computation.4 | loop fusion | flops 18874368 | bytes 47235072 | tf_op jit(solution)/shard_map/convert_element_type | solution.py:99
  693.5 45.6 %psum.31 = bf16[2,384,4]{1,2,0:T(4,128)(2,1)S(1)} all-reduce(bf16[2,384,4]{1,2,0:T(4,128)(2,1)S(1)} %copy.57), channel_id=1, replica_groups=mesh['dp'=16,'fsdp'=2] {'dp'}, use_global_device_ids=true, to_apply=%region_61.62 | all-reduce | flops 3072 | bytes 12288 | tf_op jit(solution)/shard_map/psum | solution.py:323
  739.8 262.4 %all-reduce.7.cloned.1.call-done = (bf16[2,384,768]{2,1,0:T(8,128)(2,1)}, bf16[2,384,3072]{2,1,0:T(8,128)(2,1)}, bf16[2,1536,768]{2,1,0:T(8,128)(2,1)}) async-done(((bf16[2,384,768]{2,1,0:T(8,128)(2,1)}, bf16[2,384,3072]{2,1,0:T(8,128)(2,1)}, bf16[2,1536,768]{2,1,0:T(8,128)(2,1)}), (bf16[2,384,768]{2,1,0:T(8,128)(2,1)}, bf16[2,384,3072]{2,1,0:T(8,128)(2,1)}, ...) | async-done | bytes 10616848 | tf_op jit(solution)/shard_map/psum | solution.py:320
  1009.2 22.7 %multiply_subtract_fusion.1 = (f32[2,384,3072]{2,1,0:T(8,128)}, f32[2,384,3072]{2,1,0:T(8,128)}, f32[2,384,3072]{2,1,0:T(8,128)}) fusion(f32[2,384,3072]{2,1,0:T(8,128)S(1)} %bitcast.339, bf16[2,384,3072]{2,1,0:T(8,128)(2,1)} %get-tuple-element.182, f32[2,384,3072]{2,1,0:T(8,128)} %param.46, f32[2,384,3072]{2,1,0:T(8,128)} %param.47), kind=kLoop, calls=%fused_computation.56 | loop fusion | flops 35389440 | bytes 61341696 | tf_op jit(solution)/shard_map/sub | solution.py:335
  1031.9 23.6 %multiply_subtract_fusion = (f32[2,1536,768]{2,1,0:T(8,128)}, f32[2,1536,768]{2,1,0:T(8,128)}, f32[2,1536,768]{2,1,0:T(8,128)}) fusion(f32[2,1536,768]{2,1,0:T(8,128)} %param.48, bf16[2,1536,768]{2,1,0:T(8,128)(2,1)} %get-tuple-element.183, f32[2,1536,768]{2,1,0:T(8,128)} %param.49, f32[2,1536,768]{2,1,0:T(8,128)} %param.50), kind=kLoop, calls=%fused_computation.55 | loop fusion | flops 35389440 | bytes 61341696 | tf_op jit(solution)/shard_map/sub | solution.py:335
  1055.5 517.6 %all-gather.37.cloned.1.call-done = bf16[32,384,2304]{2,1,0:T(8,128)(2,1)} async-done(((bf16[2,384,2304]{2,1,0:T(8,128)(2,1)}), bf16[32,384,2304]{2,1,0:T(8,128)(2,1)}) %all-gather.37.cloned.1.call-update) | async-done | bytes 56623120 | tf_op jit(solution)/shard_map/all_gather | solution.py:317
  1573.1 19.0 %reduce_sum.504 = bf16[2,384,2304]{2,1,0:T(8,128)(2,1)S(1)} reduce(bf16[16,2,384,2304]{3,2,1,0:T(8,128)(2,1)} %bitcast.337, bf16[]{:T(256)} %constant.276.clone.1), dimensions={0}, to_apply=%region_45.46 | reduce | flops 26542080 | bytes 60162048 | tf_op jit(solution)/shard_map/reduce_sum | solution.py:317
  1592.1 15.5 multiply_subtract_fusion.2
  (553 shorter events, 411.5 us)
Async XLA Ops:
  7.2 38.6 %all-gather.21.cloned.1.call-start = ((), (), s32[]{:S(2)}) async-start(), calls=%async_computation.9 | async-start | bytes 5308416 | tf_op jit(solution)/shard_map/all_gather | solution.py:268
  12.6 137.6 %all-gather.23.cloned.1.call-start = ((), (), s32[]{:S(2)}) async-start(), calls=%async_computation.10 | async-start | bytes 1769472 | tf_op jit(solution)/shard_map/all_gather | solution.py:269
  14.6 141.7 %all-gather.25.cloned.1.call-start = ((), (), s32[]{:S(2)}) async-start(), calls=%async_computation.11 | async-start | bytes 7077888 | tf_op jit(solution)/shard_map/all_gather | solution.py:270
  21.6 145.9 %all-gather.27.cloned.1.call-start = ((), (), s32[]{:S(2)}) async-start(), calls=%async_computation.12 | async-start | bytes 7077888 | tf_op jit(solution)/shard_map/all_gather | solution.py:271
  29.6 152.1 %all-gather.29.cloned.1.call-start = ((), (), s32[]{:S(2)}) async-start(), calls=%async_computation.13 | async-start | bytes 5308416 | tf_op jit(solution)/shard_map/all_gather | solution.py:268
  30.2 247.1 %all-gather.31.cloned.1.call-start = ((), (), s32[]{:S(2)}) async-start(), calls=%async_computation.14 | async-start | bytes 1769472 | tf_op jit(solution)/shard_map/all_gather | solution.py:269
  30.7 251.2 %all-gather.33.cloned.1.call-start = ((), (), s32[]{:S(2)}) async-start(), calls=%async_computation.15 | async-start | bytes 7077888 | tf_op jit(solution)/shard_map/all_gather | solution.py:270
  31.5 261.6 %all-gather.35.cloned.1.call-start = ((), (), s32[]{:S(2)}) async-start(), calls=%async_computation.16 | async-start | bytes 7077888 | tf_op jit(solution)/shard_map/all_gather | solution.py:271
  32.3 629.2 %reduce-scatter.10.cloned.1.call-start = ((), (), s32[]{:S(2)}) async-start(), calls=%async_computation.6 | async-start | bytes 3538944 | tf_op jit(solution)/shard_map/reduce_scatter | solution.py:303
  37.8 118.5 %copy-start.84 = (f32[768]{0:T(1024)}, f32[768]{0:T(1024)S(1)}, u32[]{:S(2)}) copy-start(f32[768]{0:T(1024)S(1)} %get-tuple-element.177) | copy-start | bytes 9220
  42.2 108.1 %copy-start.2 = (bf16[1,1024,768]{1,2,0:T(8,128)(2,1)}, bf16[1,1024,768]{1,2,0:T(8,128)(2,1)S(1)}, u32[]{:S(2)}) copy-start(bf16[1,1024,768]{1,2,0:T(8,128)(2,1)S(1)} %copy.44) | copy-start | bytes 4718596
  463.6 197.9 %reduce-scatter.14.cloned.1.call-start = ((), (), s32[]{:S(2)}) async-start(), calls=%async_computation.8 | async-start | bytes 14155776 | tf_op jit(solution)/shard_map/reduce_scatter | solution.py:309
  497.8 163.8 %reduce-scatter.12.cloned.1.call-start = ((), (), s32[]{:S(2)}) async-start(), calls=%async_computation.7 | async-start | bytes 14155776 | tf_op jit(solution)/shard_map/reduce_scatter | solution.py:306
  542.3 124.7 %reduce-scatter.8.cloned.1.call-start = ((), (), s32[]{:S(2)}) async-start(), calls=%async_computation.5 | async-start | bytes 10616832 | tf_op jit(solution)/shard_map/reduce_scatter | solution.py:300
  575.5 36.8 %slice-start.3 = ((s8[9437184]{0:T(1024)(128)(4,1)}), s8[4194304]{0:T(1024)(128)(4,1)S(1)}, s32[]{:S(2)}) async-start(s8[9437184]{0:T(1024)(128)(4,1)} %bitcast.335), calls=%async_computation.23 | async-start | bytes 8388608
  575.5 36.8 %slice-start.4 = ((s8[9437184]{0:T(1024)(128)(4,1)}), s8[1048576]{0:T(1024)(128)(4,1)S(1)}, s32[]{:S(2)}) async-start(s8[9437184]{0:T(1024)(128)(4,1)} %bitcast.335), calls=%async_computation.24 | async-start | bytes 2097152
  648.8 41.9 %reduce-scatter.16.cloned.1.call-start = ((), (), s32[]{:S(2)}) async-start(), calls=%async_computation.18 | async-start | bytes 294912
  661.4 340.8 %all-reduce.7.cloned.1.call-start = ((), (), s32[]{:S(2)}) async-start(), calls=%async_computation.19 | async-start | bytes 21233664 | tf_op jit(solution)/shard_map/psum | solution.py:320
  662.0 911.1 %all-gather.37.cloned.1.call-start = ((), (), s32[]{:S(2)}) async-start(), calls=%async_computation.17 | async-start | bytes 60162048 | tf_op jit(solution)/shard_map/all_gather | solution.py:317
  686.9 52.2 %copy-start.106 = (f32[2,384,4]{1,2,0:T(4,128)S(1)}, f32[2,384,4]{1,2,0:T(4,128)}, u32[]{:S(2)}) copy-start(f32[2,384,4]{1,2,0:T(4,128)} %param.51) | copy-start | bytes 36868
  687.0 52.2 %copy-start.138 = (f32[2,384,4]{1,2,0:T(4,128)S(1)}, f32[2,384,4]{1,2,0:T(4,128)}, u32[]{:S(2)}) copy-start(f32[2,384,4]{1,2,0:T(4,128)} %param.52) | copy-start | bytes 36868
  687.0 52.2 %copy-start.139 = (f32[2,384,4]{1,2,0:T(4,128)S(1)}, f32[2,384,4]{1,2,0:T(4,128)}, u32[]{:S(2)}) copy-start(f32[2,384,4]{1,2,0:T(4,128)} %param.53) | copy-start | bytes 36868
  687.0 315.3 %copy-start.34 = (f32[2,384,768]{2,1,0:T(8,128)S(1)}, f32[2,384,768]{2,1,0:T(8,128)}, u32[]{:S(2)}) copy-start(f32[2,384,768]{2,1,0:T(8,128)} %param.42) | copy-start | bytes 7077892
  687.0 322.1 %slice-start.6 = ((s8[9437184]{0:T(1024)(128)(4,1)}), s8[1048576]{0:T(1024)(128)(4,1)S(1)}, s32[]{:S(2)}) async-start(s8[9437184]{0:T(1024)(128)(4,1)} %bitcast.338), calls=%async_computation.26 | async-start | bytes 2097152
  (162 other events, 1038.7 us)
Sparse Core Ops, SparseCore 0:
  12.8 15.3 all-gather.20
  30.3 10.3 all-gather.22
  42.9 15.6 all-gather.24
  60.5 15.6 all-gather.26
  78.1 13.8 all-gather.28
  94.0 10.3 all-gather.30
  106.6 15.5 all-gather.32
  124.3 15.5 all-gather.34
  463.7 11.6 reduce-scatter.9
  497.9 19.4 reduce-scatter.13
  542.5 19.8 reduce-scatter.11
  648.9 18.0 reduce-scatter.7
  669.8 8.7 reduce-scatter.15
  684.9 317.3 all-reduce.6
  1005.3 567.7 all-gather.36
